TPU v7x, 256 devices: a whole 4x4x8 slice. The times are simulated.
256 devices in a mesh: gx: 32 (over y, x, core), gz: 8 (over z).
Axes of the slice: x: 4, y: 4, z: 8, core: 2. Of those that a mesh axis runs over, the one named last changes fastest.
Arguments:
- charge: float32 [512, 128, 128], P('gx', 'gz'), may hold values from -4 to 4
- region_codes: int32 [512, 128, 128], P('gx', 'gz'), may hold values from 0 to 7
- eps_table: float32 [8], replicated, may hold values from 0.025 to 1
- screen_table: float32 [8], replicated, may hold values from 0.005 to 0.05
Outputs:
- potential: float32 [512, 128, 128], P('gx', 'gz')
All inputs are finite; a program needn't handle non-finite values.
Results may differ from a plain program's by a relative error of at most 0.0001.
Values sent between devices are 32-bit elements; how exact they have to be, the bound alone decides.
A program may use at most 128 MiB of HBM per device.

v0:
```python
import jax
import jax.numpy as jnp
from jax import lax
from jax.experimental import pallas as pl
from jax.experimental.pallas import tpu as pltpu
from jax.sharding import PartitionSpec as P

OMEGA = 0.8
SWEEPS = 8
LAST = 6
F32 = jnp.float32
MESH = pl.DeviceIdType.MESH


def iota(shape, dim):
    return lax.broadcasted_iota(jnp.int32, shape, dim)


def roll(v, shift, axis):
    size = v.shape[axis]
    return pltpu.roll(v, shift % size, axis)


class Level:
    def __init__(self, index, refs, whole, slab):
        (self.E, self.S, self.WXM, self.WXP, self.WYM, self.WYP, self.WZ, self.D, self.A, self.M, self.F, self.U, self.R, self.Y,
         self.V, self.C) = refs
        self.index, self.whole, self.n = index, whole, slab
        self.Z, self.X = self.S.shape[0], self.S.shape[1]
        self.mask = None

    @staticmethod
    def scratch(Z, X):
        sizes = (Z + 2, Z, Z, Z, Z, Z, Z + 1, Z, Z + 1, Z, Z, Z, Z, Z, Z + 2, Z + 2)
        return [pltpu.VMEM((s, X, 128), F32) for s in sizes]


def loop(count, body):
    def step(i, carry):
        body(i)
        return carry

    lax.fori_loop(0, count, step, 0)


def couplings(lev, z0, n):
    h = 0.5 ** lev.index * 0.5
    sh = 2 ** lev.index
    X = lev.X
    e = lev.E[pl.ds(z0 + 1, n)]
    lane = iota((n, X, 128), 2)
    first, last = lane < sh, lane >= 128 - sh
    up, down = roll(e, 1, 1), roll(e, -1, 1)
    if lev.whole:
        row = iota((n, X, 128), 1)
        up, down = jnp.where(row == 0, 0.0, up), jnp.where(row == X - 1, 0.0, down)
    left, right = jnp.where(first, 0.0, roll(e, sh, 2)), jnp.where(last, 0.0, roll(e, -sh, 2))
    wxm, wxp, wym, wyp = h * (e + up), h * (e + down), h * (e + left), h * (e + right)
    wzm, wzp = h * (e + lev.E[pl.ds(z0, n)]), h * (e + lev.E[pl.ds(z0 + 2, n)])
    lev.D[pl.ds(z0, n)] = wxm + wxp + wzm + wzp + wym + wyp + lev.S[pl.ds(z0, n)]
    if lev.whole:
        wxm, wxp = jnp.where(row == 0, 0.0, wxm), jnp.where(row == X - 1, 0.0, wxp)
    lev.WXM[pl.ds(z0, n)] = wxm
    lev.WXP[pl.ds(z0, n)] = wxp
    lev.WYM[pl.ds(z0, n)] = jnp.where(first, 0.0, wym)
    lev.WYP[pl.ds(z0, n)] = jnp.where(last, 0.0, wyp)
    lev.WZ[pl.ds(z0, n)] = wzm
    return wzp


def lateral(lev, u, z0, n):
    sh = 2 ** lev.index
    return (
        lev.WXM[pl.ds(z0, n)] * roll(u, 1, 1)
        + lev.WXP[pl.ds(z0, n)] * roll(u, -1, 1)
        + lev.WYM[pl.ds(z0, n)] * roll(u, sh, 2)
        + lev.WYP[pl.ds(z0, n)] * roll(u, -sh, 2)
    )


def steps_of(count):
    for s in (8, 4, 2):
        if count % s == 0:
            return s
    return 1


def prepare(lev):
    Z, X, n = lev.Z, lev.X, lev.n
    zero = jnp.zeros((1, X, 128), F32)
    lev.E[0:1] = zero
    lev.E[Z + 1 : Z + 2] = zero
    loop(Z // n, lambda i: couplings(lev, i * n, n))
    lev.WZ[0:1] = zero
    lev.WZ[Z : Z + 1] = zero
    lev.A[Z : Z + 1] = zero
    s = steps_of(Z)

    def body(i, m):
        for j in range(s):
            z = i * s + j
            w = lev.WZ[z]
            a = w * m
            m = 1.0 / (lev.D[z] - w * a)
            lev.A[z] = a
            lev.M[z] = m
        return m

    lax.fori_loop(0, Z // s, body, jnp.zeros((X, 128), F32))


def sweep(lev, src, finish):
    Z, X = lev.Z, lev.X
    s = steps_of(Z)

    def forward(i, y):
        for j in range(s):
            z = i * s + j
            y = src[z] + lev.A[z] * y
            lev.Y[z] = y
        return y

    def backward(i, x):
        for j in range(s):
            z = Z - 1 - (i * s + j)
            x = lev.M[z] * lev.Y[z] + lev.A[z + 1] * x
            finish(z, x)
        return x

    lax.fori_loop(0, Z // s, forward, jnp.zeros((X, 128), F32))
    lax.fori_loop(0, Z // s, backward, jnp.zeros((X, 128), F32))


def pair_lanes(v, index):
    sh = 2 ** index
    lane = iota(v.shape, v.ndim - 1)
    other = jnp.where((lane & sh) == 0, roll(v, -sh, v.ndim - 1), roll(v, sh, v.ndim - 1))
    return v + other


def halve(v, index, tmp):
    n, X = v.shape[0], v.shape[1]
    v = v.reshape(n // 2, 2, X, 128)
    v = pair_lanes(v[:, 0] + v[:, 1], index)
    tmp[0 : n // 2, 0:X, :] = v
    return 0.125 * (tmp[0 : n // 2, pl.ds(0, X // 2, stride=2), :] + tmp[0 : n // 2, pl.ds(1, X // 2, stride=2), :])


def pre(lev):
    def finish(z, x):
        lev.U[z] = OMEGA * x

    sweep(lev, lev.F, finish)
    n = lev.n

    def body(i):
        z0 = i * n
        r = (1.0 - OMEGA) * lev.F[pl.ds(z0, n)] + lateral(lev, lev.U[pl.ds(z0, n)], z0, n)
        if lev.mask is not None:
            r = jnp.where(lev.mask[None] > 0, r, 0.0)
        lev.R[pl.ds(z0, n)] = r

    loop(lev.Z // n, body)


def post(lev):
    n, Z = lev.n, lev.Z
    zero = jnp.zeros((1, lev.X, 128), F32)
    lev.V[0:1] = zero
    lev.V[Z + 1 : Z + 2] = zero

    def body(i):
        z0 = i * n
        v = lev.V[pl.ds(z0 + 1, n)]
        around = lateral(lev, v, z0, n) + lev.WZ[pl.ds(z0, n)] * lev.V[pl.ds(z0, n)] + lev.WZ[pl.ds(z0 + 1, n)] * lev.V[pl.ds(z0 + 2, n)]
        r = lev.R[pl.ds(z0, n)] - (lev.D[pl.ds(z0, n)] * v - around)
        if lev.mask is not None:
            r = jnp.where(lev.mask[None] > 0, r, 0.0)
        lev.F[pl.ds(z0, n)] = r

    loop(Z // n, body)

    def finish(z, x):
        lev.C[z + 1] = lev.U[z] + lev.V[z + 1] + OMEGA * x

    sweep(lev, lev.F, finish)


def coarsest(lev):
    Z = lev.Z

    def first(z, x):
        lev.U[z] = OMEGA * x

    def again(z, x):
        lev.U[z] = (1.0 - OMEGA) * lev.U[z] + OMEGA * x

    def last(z, x):
        lev.C[z + 1] = (1.0 - OMEGA) * lev.U[z] + OMEGA * x

    sweep(lev, lev.F, first)

    def once(finish):
        lev.R[...] = lev.F[...] + lateral(lev, lev.U[...], 0, Z)
        sweep(lev, lev.R, finish)

    loop(SWEEPS - 2, lambda i: once(again))
    once(last)


def spread_rows(dst, z, c, rows):
    for source, count, target in rows:
        part = c[source : source + count]
        for k in range(2):
            for j in range(2):
                dst[z + k, pl.ds(target + j, count, stride=2), :] = part


def kernel(ngx, ngz, *refs):
    codes, charge, eps_t, scr_t, out = refs[:5]
    refs = list(refs[5:])

    def take(count):
        got = refs[:count]
        del refs[:count]
        return got

    l0 = Level(0, take(16), False, 4)
    l1 = Level(1, take(16), False, 8)
    l2 = Level(2, take(16), False, 8)
    l3 = Level(3, take(16), True, 4)
    l4 = Level(4, take(16), True, 4)
    l5 = Level(5, take(16), True, 4)
    l6 = Level(6, take(16), True, 2)
    (tmp, xs, xr, zs, zr, ds, dr, es, f1, red, post_red, ub, rm, ra, av, bv, es3, f3) = take(18)
    (s_r1, r_r1, s_es, r_es, s_f1, r_f1, s_red, r_red, s_post, r_post, s_e3, r_e3, s_f3, r_f3) = take(14)

    gx, gz = lax.axis_index("gx"), lax.axis_index("gz")

    def gx_at(k):
        return lax.rem(gx + (k + ngx), ngx)

    def gz_at(k):
        return lax.rem(gz + (k + ngz), ngz)

    def remote(src, dst, ss, rs, tx, tz):
        return pltpu.make_async_remote_copy(src, dst, ss, rs, device_id=(tx, tz), device_id_type=MESH)

    barrier = pltpu.get_barrier_semaphore()

    def hello(tx, tz):
        pl.semaphore_signal(barrier, 1, device_id=(tx, tz), device_id_type=MESH)

    loop(ngz - 1, lambda k: hello(gx, gz_at(k + 1)))
    loop(ngz, lambda k: hello(gx_at(1), gz_at(k)))
    loop(ngz, lambda k: hello(gx_at(-1), gz_at(k)))
    loop(ngx - 3, lambda k: hello(gx_at(k + 2), gz))

    row24, row16 = iota((24, 128), 0), iota((16, 128), 0)
    has_right, has_left = gx < ngx - 1, gx > 0
    lane = iota((1, 8, 128), 2)

    def look(i):
        c = codes[pl.ds(i, 16, stride=16), :]
        e = jnp.zeros((16, 128), F32)
        s = jnp.zeros((16, 128), F32)
        for k in range(eps_t.shape[0]):
            e = jnp.where(c == k, eps_t[k], e)
            s = jnp.where(c == k, scr_t[k], s)
        l0.E[i + 1, 0:16, :] = e
        l0.S[i, 0:16, :] = s
        l0.F[i, 0:16, :] = charge[pl.ds(i, 16, stride=16), :]

    loop(16, look)

    xs[0, :, 0:2, :] = l0.E[1:17, 14:16, :]
    xs[0, :, 2:3, :] = l0.S[:, 15:16, :]
    xs[0, :, 3:4, :] = l0.F[:, 15:16, :]
    xs[1, :, 0:2, :] = l0.E[1:17, 0:2, :]
    xs[1, :, 2:3, :] = l0.S[:, 0:1, :]
    xs[1, :, 3:4, :] = l0.F[:, 0:1, :]
    zs[0] = l0.E[16, 0:16, :]
    zs[1] = l0.E[1, 0:16, :]
    ds[0] = l0.E[16, 8:16, :]
    ds[1] = l0.E[16, 0:8, :]
    ds[2] = l0.E[1, 8:16, :]
    ds[3] = l0.E[1, 0:8, :]

    def r1_copies():
        return [
            remote(xs.at[0], xr.at[0], s_r1.at[0], r_r1.at[0], gx_at(1), gz),
            remote(xs.at[1], xr.at[1], s_r1.at[1], r_r1.at[1], gx_at(-1), gz),
            remote(zs.at[0], zr.at[0], s_r1.at[2], r_r1.at[2], gx, gz_at(1)),
            remote(zs.at[1], zr.at[1], s_r1.at[3], r_r1.at[3], gx, gz_at(-1)),
            remote(ds.at[0], dr.at[0], s_r1.at[4], r_r1.at[4], gx_at(1), gz_at(1)),
            remote(ds.at[1], dr.at[1], s_r1.at[5], r_r1.at[5], gx_at(-1), gz_at(1)),
            remote(ds.at[2], dr.at[2], s_r1.at[6], r_r1.at[6], gx_at(1), gz_at(-1)),
            remote(ds.at[3], dr.at[3], s_r1.at[7], r_r1.at[7], gx_at(-1), gz_at(-1)),
        ]

    pl.semaphore_wait(barrier, 3 * ngz - 1 + ngx - 3)
    for copy in r1_copies():
        copy.start()

    def pack2(v):
        v = v.reshape(4, 2, 8, 128)
        return jnp.where((lane & 1) == 0, v[:, 0], v[:, 1])

    es[0, gz, 0:4] = pack2(halve(l0.E[1:17, 0:16, :], 0, tmp))
    es[0, gz, 4:8] = pack2(halve(l0.S[:, 0:16, :], 0, tmp))

    def to_lines(buf, ss, rs, act):
        mine = buf.at[0, gz]

        def go(slot, k, tx):
            act(remote(mine, buf.at[slot, gz], ss.at[slot, k], rs.at[slot, gz], tx, gz_at(k)))

        loop(ngz - 1, lambda k: go(0, k + 1, gx))
        loop(ngz, lambda k: go(2, k, gx_at(1)))
        loop(ngz, lambda k: go(1, k, gx_at(-1)))

    def from_lines(buf, ss, rs):
        mine = buf.at[0, gz]

        def get(slot, k):
            p = gz_at(k)
            remote(mine, buf.at[slot, p], ss.at[slot, k], rs.at[slot, p], gx, gz_at(1)).wait_recv()

        loop(ngz - 1, lambda k: get(0, k + 1))
        loop(ngz, lambda k: get(1, k))
        loop(ngz, lambda k: get(2, k))

    to_lines(es, s_es, r_es, lambda c: c.start())

    for copy in r1_copies():
        copy.wait_recv()

    above, below = gz > 0, gz < ngz - 1
    zero16 = jnp.zeros((16, 24, 128), F32)
    l0.E[0:1] = zero16[0:1]
    l0.E[17:18] = zero16[0:1]
    l0.E[1:17, 16:24, :] = zero16[:, 0:8]
    l0.S[:, 16:24, :] = jnp.ones((16, 8, 128), F32)
    l0.F[:, 16:24, :] = zero16[:, 0:8]
    l0.E[1:17, 22:24, :] = jnp.where(has_left, xr[0, :, 0:2, :], 0.0)
    l0.S[:, 23:24, :] = jnp.where(has_left, xr[0, :, 2:3, :], 1.0)
    l0.F[:, 23:24, :] = jnp.where(has_left, xr[0, :, 3:4, :], 0.0)
    l0.E[1:17, 16:18, :] = jnp.where(has_right, xr[1, :, 0:2, :], 0.0)
    l0.S[:, 16:17, :] = jnp.where(has_right, xr[1, :, 2:3, :], 1.0)
    l0.F[:, 16:17, :] = jnp.where(has_right, xr[1, :, 3:4, :], 0.0)
    l0.E[0, 0:16, :] = jnp.where(above, zr[0], 0.0)
    l0.E[17, 0:16, :] = jnp.where(below, zr[1], 0.0)
    l0.E[0, 23:24, :] = jnp.where(above & has_left, dr[0, 7:8, :], 0.0)
    l0.E[0, 16:17, :] = jnp.where(above & has_right, dr[1, 0:1, :], 0.0)
    l0.E[17, 23:24, :] = jnp.where(below & has_left, dr[2, 7:8, :], 0.0)
    l0.E[17, 16:17, :] = jnp.where(below & has_right, dr[3, 0:1, :], 0.0)

    for i in range(4):
        wzp = couplings(l0, i * 4, 4)
    l0.WZ[16:17] = wzp[3:4]

    m = 1.0 / l0.D[0]
    l0.M[0] = m
    for z in range(1, 15):
        w = l0.WZ[z]
        a = w * m
        m = 1.0 / (l0.D[z] - w * a)
        l0.A[z] = a
        l0.M[z] = m
    lead = jnp.where(above, l0.WZ[0], 0.0)
    tail = l0.WZ[15]

    y = lead
    av[0] = y
    for z in range(1, 15):
        y = l0.A[z] * y
        av[z] = y
    x = l0.M[14] * y
    b = l0.M[14] * tail
    av[14] = x
    bv[14] = b
    for z in range(13, -1, -1):
        x = l0.M[z] * av[z] + l0.A[z + 1] * x
        b = l0.A[z + 1] * b
        av[z] = x
        bv[z] = b

    def inner(src):
        y = src[0]
        l0.Y[0] = y
        for z in range(1, 15):
            y = src[z] + l0.A[z] * y
            l0.Y[z] = y
        x = l0.M[14] * y
        l0.Y[14] = x
        for z in range(13, -1, -1):
            x = l0.M[z] * l0.Y[z] + l0.A[z + 1] * x
            l0.Y[z] = x

    inner(l0.F)

    def put(k, v):
        red[gz, pl.ds(k * 18, 17), :] = v[0:17]
        red[gz, pl.ds(k * 18 + 17, 1), :] = v[23:24]

    put(0, tail * av[14])
    put(1, l0.D[15] - tail * bv[14])
    put(2, lead * av[0])
    put(3, l0.F[15] + tail * l0.Y[14])
    put(4, lead * l0.Y[0])

    def gather(buf, ss, rs, act):
        loop(ngz - 1, lambda k: act(remote(buf.at[gz], buf.at[gz], ss.at[k + 1], rs.at[gz], gx, gz_at(k + 1))))

    def gathered(buf, ss, rs):
        def get(k):
            p = gz_at(k)
            remote(buf.at[gz], buf.at[p], ss.at[k], rs.at[p], gx, p).wait_recv()

        loop(ngz - 1, lambda k: get(k + 1))

    gather(red, s_red, r_red, lambda c: c.start())

    from_lines(es, s_es, r_es)
    mask1 = jnp.where(row24 < 8, 1.0, jnp.where(row24 < 16, jnp.where(has_right, 1.0, 0.0), jnp.where(has_left, 1.0, 0.0)))
    mask2 = jnp.where(
        row16 < 4,
        1.0,
        jnp.where(row16 < 8, jnp.where(has_right, 1.0, 0.0), jnp.where(row16 < 12, 0.0, jnp.where(has_left, 1.0, 0.0))),
    )
    l1.mask, l2.mask = mask1, mask2

    def unpack2(v):
        even = jnp.where((lane & 1) == 0, v, roll(v, 1, 2))
        odd = jnp.where((lane & 1) == 1, v, roll(v, -1, 2))
        return jnp.stack([even, odd], axis=1).reshape(2 * v.shape[0], 8, 128)

    here = (None, has_right, has_left)

    def place(buf, start, dst, offset, outside):
        for slot in range(3):

            def body(p, slot=slot):
                v = unpack2(buf[slot, p, start : start + 4])
                if slot:
                    v = jnp.where(here[slot], v, outside)
                dst[pl.ds(p * 8 + offset, 8), slot * 8 : slot * 8 + 8, :] = v

            loop(ngz, body)

    place(es, 0, l1.E, 1, 0.0)
    place(es, 4, l1.S, 0, 1.0)

    def coarsen(src, offset, fine, coarse, dst, dst_offset, split):
        n = fine.n

        def body(i):
            v = halve(src[pl.ds(i * n + offset, n)], fine.index, tmp)
            at = pl.ds(i * (n // 2) + dst_offset, n // 2)
            if split:
                dst[at, 0:8, :] = v[:, 0:8]
                dst[at, 12:16, :] = v[:, 8:12]
            else:
                dst[at] = v

        loop(fine.Z // n, body)

    def filler(ref, value):
        ref[:, 8:12, :] = jnp.full((ref.shape[0], 4, 128), value, F32)

    filler(l2.E, 0.0)
    filler(l2.S, 1.0)
    filler(l2.F, 0.0)
    coarsen(l1.E, 1, l1, l2, l2.E, 1, True)
    coarsen(l1.S, 0, l1, l2, l2.S, 0, True)

    lane3 = iota((4, 2, 128), 2)

    def pack4(src, offset, buf, first):
        for i in range(2):
            v = halve(src[i * 16 + offset : i * 16 + offset + 16], 2, tmp)[:, 0:2]
            tmp[i * 8 : i * 8 + 8, 32:34, :] = v
        v = tmp[0:16, 32:34, :].reshape(4, 4, 2, 128)
        k = (lane3 >> 1) & 3
        v = jnp.where(k == 0, v[:, 0], jnp.where(k == 1, v[:, 1], jnp.where(k == 2, v[:, 2], v[:, 3])))
        for zz in range(4):
            buf[gx, first + zz * 2 : first + zz * 2 + 2, :] = v[zz]

    pack4(l2.E, 1, es3, 0)
    pack4(l2.S, 0, es3, 8)

    def spread(buf, ss, rs, act):
        loop(ngx - 1, lambda k: act(remote(buf.at[gx], buf.at[gx], ss.at[k + 1], rs.at[gx], gx_at(k + 1), gz)))

    def collected(buf, ss, rs):
        def get(k):
            p = gx_at(k)
            remote(buf.at[gx], buf.at[p], ss.at[k], rs.at[p], p, gz).wait_recv()

        loop(ngx - 1, lambda k: get(k + 1))

    spread(es3, s_e3, r_e3, lambda c: c.start())

    gathered(red, s_red, r_red)

    def got(p, k):
        return red[p, pl.ds(k * 18, 18), :]

    m, y = None, None
    for p in range(ngz):
        diag, right = got(p, 1), got(p, 3)
        if p + 1 < ngz:
            diag, right = diag - got(p + 1, 2), right + got(p + 1, 4)
        if p:
            c = got(p, 0)
            a = c * m
            diag, right = diag - c * a, right + a * y
            ra[p] = a
        m, y = 1.0 / diag, right
        rm[p] = m
        ub[p + 1, 0:18, :] = y
    x = m * y
    for p in range(ngz - 1, -1, -1):
        if p + 1 < ngz:
            x = rm[p] * ub[p + 1, 0:18, :] + ra[p + 1] * x
        ub[p + 1, 0:17, :] = x[0:17]
        ub[p + 1, 23:24, :] = x[17:18]
        ub[p + 1, 17:23, :] = jnp.zeros((6, 128), F32)
    ub[0] = jnp.zeros((24, 128), F32)

    before, own = ub[gz], ub[gz + 1]
    for z in range(15):
        l0.U[z] = OMEGA * (l0.Y[z] + av[z] * before + bv[z] * own)
    l0.U[15] = OMEGA * own

    def first_residual(i):
        z0 = i * 4
        l0.R[pl.ds(z0, 4)] = (1.0 - OMEGA) * l0.F[pl.ds(z0, 4)] + lateral(l0, l0.U[pl.ds(z0, 4)], z0, 4)

    loop(4, first_residual)
    f1[0, gz] = pack2(halve(l0.R[:, 0:16, :], 0, tmp))
    to_lines(f1, s_f1, r_f1, lambda c: c.start())

    prepare(l1)
    prepare(l2)

    lane32 = iota((32, 128), 1)

    def swap(v, s):
        return jnp.where((lane32 & s) == 0, roll(v, -s, 1), roll(v, s, 1))

    def place4(buf, rows, first, dst, offset):
        for zz in range(4):
            for xp in range(2):
                v = buf[:, first + zz * 2 + xp, :]
                w = swap(v, 2)
                for k0 in range(2):
                    v1 = jnp.where(((lane32 >> 1) & 1) == k0, v, w)
                    w1 = swap(v1, 4)
                    for k1 in range(2):
                        v2 = jnp.where(((lane32 >> 2) & 1) == k1, v1, w1)
                        dst[offset + zz * 4 + k1 * 2 + k0, pl.ds(xp, ngx, stride=2), :] = v2

    from_lines(f1, s_f1, r_f1)
    place(f1, 0, l1.F, 0, 0.0)
    pre(l1)
    coarsen(l1.R, 0, l1, l2, l2.F, 0, True)
    pre(l2)
    pack4(l2.R, 0, f3, 0)
    spread(f3, s_f3, r_f3, lambda c: c.start())

    collected(es3, s_e3, r_e3)
    place4(es3, 16, 0, l3.E, 1)
    place4(es3, 16, 8, l3.S, 0)
    deep = [l3, l4, l5, l6]
    for fine, coarse in zip(deep[:-1], deep[1:]):
        coarsen(fine.E, 1, fine, coarse, coarse.E, 1, False)
        coarsen(fine.S, 0, fine, coarse, coarse.S, 0, False)
    for lev in deep:
        prepare(lev)

    collected(f3, s_f3, r_f3)
    place4(f3, 8, 0, l3.F, 0)
    for fine, coarse in zip(deep[:-1], deep[1:]):
        pre(fine)
        coarsen(fine.R, 0, fine, coarse, coarse.F, 0, False)
    coarsest(l6)
    for fine, coarse in zip(deep[-2::-1], deep[:0:-1]):
        loop(coarse.Z, lambda z, fine=fine, coarse=coarse: spread_rows(fine.V, 2 * z + 1, coarse.C[z + 1], ((0, coarse.X, 0),)))
        post(fine)

    def down3(z):
        c = pltpu.roll(l3.C[z + 1], lax.rem(2 * (ngx - gx), 2 * ngx), 0)
        spread_rows(l2.V, 2 * z + 1, c, ((0, 4, 0), (62, 2, 12)))

    filler(l2.V, 0.0)
    loop(l3.Z, down3)

    def clear(i):
        l2.V[i + 1] = jnp.where(mask2 > 0, l2.V[i + 1], 0.0)

    loop(l2.Z, clear)
    post(l2)
    loop(l2.Z, lambda z: spread_rows(l1.V, 2 * z + 1, l2.C[z + 1], ((0, 4, 0), (4, 4, 8), (12, 4, 16))))
    post(l1)
    l1.C[0] = jnp.zeros((24, 128), F32)
    l1.C[l1.Z + 1] = jnp.zeros((24, 128), F32)

    for i in range(10):
        c = l1.C[gz * 8 + i]
        for z in (2 * i - 1, 2 * i):
            if 0 <= z < 18:
                for j in range(2):
                    l0.V[z, pl.ds(j, 8, stride=2), :] = c[0:8]
                l0.V[z, 16:17, :] = c[8:9]
                l0.V[z, 17:23, :] = jnp.zeros((6, 128), F32)
                l0.V[z, 23:24, :] = c[23:24]

    def second_residual(i):
        z0 = i * 4
        v = l0.V[pl.ds(z0 + 1, 4)]
        around = lateral(l0, v, z0, 4) + l0.WZ[pl.ds(z0, 4)] * l0.V[pl.ds(z0, 4)] + l0.WZ[pl.ds(z0 + 1, 4)] * l0.V[pl.ds(z0 + 2, 4)]
        l0.F[pl.ds(z0, 4)] = l0.R[pl.ds(z0, 4)] - (l0.D[pl.ds(z0, 4)] * v - around)

    loop(4, second_residual)
    inner(l0.F)
    post_red[gz, 0:16, :] = (l0.F[15] + tail * l0.Y[14])[0:16]
    post_red[gz, 16:32, :] = (lead * l0.Y[0])[0:16]
    gather(post_red, s_post, r_post, lambda c: c.start())
    gathered(post_red, s_post, r_post)
    y = None
    for p in range(ngz):
        right = post_red[p, 0:16, :]
        if p + 1 < ngz:
            right = right + post_red[p + 1, 16:32, :]
        if p:
            right = right + ra[p, 0:16, :] * y
        y = right
        ub[p + 1, 0:16, :] = y
    x = rm[ngz - 1, 0:16, :] * y
    for p in range(ngz - 1, -1, -1):
        if p + 1 < ngz:
            x = rm[p, 0:16, :] * ub[p + 1, 0:16, :] + ra[p + 1, 0:16, :] * x
        ub[p + 1, 0:16, :] = x
    before, own = ub[gz, 0:16, :], ub[gz + 1, 0:16, :]
    for z in range(16):
        if z < 15:
            x = l0.Y[z, 0:16, :] + av[z, 0:16, :] * before + bv[z, 0:16, :] * own
        else:
            x = own
        out[pl.ds(z, 16, stride=16), :] = l0.U[z, 0:16, :] + l0.V[z + 1, 0:16, :] + OMEGA * x

    for copy in r1_copies():
        copy.wait_send()
    to_lines(es, s_es, r_es, lambda c: c.wait_send())
    to_lines(f1, s_f1, r_f1, lambda c: c.wait_send())
    gather(red, s_red, r_red, lambda c: c.wait_send())
    gather(post_red, s_post, r_post, lambda c: c.wait_send())
    spread(es3, s_e3, r_e3, lambda c: c.wait_send())
    spread(f3, s_f3, r_f3, lambda c: c.wait_send())


def solution(mesh):
    ngx, ngz = mesh.shape["gx"], mesh.shape["gz"]

    def per_device(charge, codes, eps_table, screen_table):
        nx, nz, ny = charge.shape
        whole_z, whole_x = nz * ngz, nx * ngx
        levels = [
            (nz, 24),
            (whole_z // 2, 24),
            (whole_z // 4, 16),
            (whole_z // 8, whole_x // 8),
            (whole_z // 16, whole_x // 16),
            (whole_z // 32, whole_x // 32),
            (whole_z // 64, whole_x // 64),
        ]
        scratch = []
        for Z, X in levels:
            scratch += Level.scratch(Z, X)
        vm = lambda *shape: pltpu.VMEM(shape, F32)
        scratch += [
            vm(16, 64, 128),
            vm(2, 16, 4, 128),
            vm(2, 16, 4, 128),
            vm(2, 16, 128),
            vm(2, 16, 128),
            vm(4, 8, 128),
            vm(4, 8, 128),
            vm(3, ngz, 8, 8, 128),
            vm(3, ngz, 4, 8, 128),
            vm(ngz, 96, 128),
            vm(ngz, 32, 128),
            vm(ngz + 1, 24, 128),
            vm(ngz, 18, 128),
            vm(ngz, 18, 128),
            vm(16, 24, 128),
            vm(16, 24, 128),
            vm(ngx, 16, 128),
            vm(ngx, 8, 128),
        ]
        for shape in ((8,), (3, ngz), (3, ngz), (ngz,), (ngz,), (ngx,), (ngx,)):
            scratch += [pltpu.SemaphoreType.DMA(shape)] * 2
        result = pl.pallas_call(
            lambda *refs: kernel(ngx, ngz, *refs),
            out_shape=jax.ShapeDtypeStruct((nx * nz, ny), F32),
            in_specs=[
                pl.BlockSpec(memory_space=pltpu.VMEM),
                pl.BlockSpec(memory_space=pltpu.VMEM),
                pl.BlockSpec(memory_space=pltpu.SMEM),
                pl.BlockSpec(memory_space=pltpu.SMEM),
            ],
            out_specs=pl.BlockSpec(memory_space=pltpu.VMEM),
            scratch_shapes=scratch,
            compiler_params=pltpu.CompilerParams(collective_id=0, has_side_effects=True, vmem_limit_bytes=56 << 20),
            name="vcycle",
        )(codes.reshape(nx * nz, ny), charge.reshape(nx * nz, ny), eps_table, screen_table)
        return result.reshape(nx, nz, ny)

    return jax.shard_map(
        per_device,
        mesh=mesh,
        in_specs=(P("gx", "gz", None), P("gx", "gz", None), P(), P()),
        out_specs=P("gx", "gz", None),
        check_vma=False,
    )
```

profile of v0, /device:TPU:1, one launch (start us, length us, event | category | flops | bytes accessed | tf_op | source)
XLA Modules:
  0.0 82.0 jit_solution(15612267388909659761)
XLA Ops:
  0.0 80.5 %vcycle.1 = f32[256,128]{1,0:T(8,128)} custom-call(s32[256,128]{1,0:T(8,128)} %bitcast.4, f32[256,128]{1,0:T(8,128)} %bitcast.5, f32[8]{0:T(128)} %refs_2_.1, f32[8]{0:T(128)} %refs_3_.1), custom_call_target="tpu_custom_call" | custom-call | tf_op jit(solution)/shard_map/vcycle/pallas_call | solution.py:704
  80.5 1.6 %copy.6 = f32[16,16,128]{2,1,0:T(8,128)} copy(f32[16,16,128]{2,1,0:T(8,128)} %bitcast.3) | data formatting | bytes 262144
where the time goes:
time: 82.1 us; the launch traced here: 82 us
  Pallas kernels  80.5 us (98%)
  local copies, waits for them, and re-layouts  1.57 us (2%)
    pallas_call x1, Pallas kernels, per_device(): pl.pallas_call(lambda *refs: kernel(ngx, ngz, *refs), out_shape=jax.Shape...  80.5 us

commit v1 on v0

--- a/solution.py
+++ b/solution.py
@@ -41,6 +41,11 @@
         return carry
 
     lax.fori_loop(0, count, step, 0)
+
+
+def unrolled(count, body):
+    for i in range(count):
+        body(i)
 
 
 def couplings(lev, z0, n):
@@ -90,7 +95,7 @@
     zero = jnp.zeros((1, X, 128), F32)
     lev.E[0:1] = zero
     lev.E[Z + 1 : Z + 2] = zero
-    loop(Z // n, lambda i: couplings(lev, i * n, n))
+    (loop if Z // n > 8 else unrolled)(Z // n, lambda i: couplings(lev, i * n, n))
     lev.WZ[0:1] = zero
     lev.WZ[Z : Z + 1] = zero
     lev.A[Z : Z + 1] = zero
@@ -138,12 +143,13 @@
     return v + other
 
 
-def halve(v, index, tmp):
+def halve(v, index, tmp, at=0):
     n, X = v.shape[0], v.shape[1]
     v = v.reshape(n // 2, 2, X, 128)
     v = pair_lanes(v[:, 0] + v[:, 1], index)
-    tmp[0 : n // 2, 0:X, :] = v
-    return 0.125 * (tmp[0 : n // 2, pl.ds(0, X // 2, stride=2), :] + tmp[0 : n // 2, pl.ds(1, X // 2, stride=2), :])
+    part = slice(at, at + n // 2)
+    tmp[part, 0:X, :] = v
+    return 0.125 * (tmp[part, pl.ds(0, X // 2, stride=2), :] + tmp[part, pl.ds(1, X // 2, stride=2), :])
 
 
 def pre(lev):
@@ -160,7 +166,7 @@
             r = jnp.where(lev.mask[None] > 0, r, 0.0)
         lev.R[pl.ds(z0, n)] = r
 
-    loop(lev.Z // n, body)
+    unrolled(lev.Z // n, body)
 
 
 def post(lev):
@@ -178,7 +184,7 @@
             r = jnp.where(lev.mask[None] > 0, r, 0.0)
         lev.F[pl.ds(z0, n)] = r
 
-    loop(Z // n, body)
+    unrolled(Z // n, body)
 
     def finish(z, x):
         lev.C[z + 1] = lev.U[z] + lev.V[z + 1] + OMEGA * x
@@ -217,7 +223,7 @@
 
 
 def kernel(ngx, ngz, *refs):
-    codes, charge, eps_t, scr_t, out = refs[:5]
+    codes_in, charge_in, eps_t, scr_t, out = refs[:5]
     refs = list(refs[5:])
 
     def take(count):
@@ -232,7 +238,7 @@
     l4 = Level(4, take(16), True, 4)
     l5 = Level(5, take(16), True, 4)
     l6 = Level(6, take(16), True, 2)
-    (tmp, xs, xr, zs, zr, ds, dr, es, f1, red, post_red, ub, rm, ra, av, bv, es3, f3) = take(18)
+    (tmp, codes, charge, s_in, xs, xr, zs, zr, ds, dr, es, f1, red, post_red, ub, rm, ra, av, bv, es3, f3) = take(21)
     (s_r1, r_r1, s_es, r_es, s_f1, r_f1, s_red, r_red, s_post, r_post, s_e3, r_e3, s_f3, r_f3) = take(14)
 
     gx, gz = lax.axis_index("gx"), lax.axis_index("gz")
@@ -245,6 +251,10 @@
 
     def remote(src, dst, ss, rs, tx, tz):
         return pltpu.make_async_remote_copy(src, dst, ss, rs, device_id=(tx, tz), device_id_type=MESH)
+
+    inputs = (pltpu.make_async_copy(codes_in, codes, s_in.at[0]), pltpu.make_async_copy(charge_in, charge, s_in.at[1]))
+    for copy in inputs:
+        copy.start()
 
     barrier = pltpu.get_barrier_semaphore()
 
@@ -259,19 +269,24 @@
     row24, row16 = iota((24, 128), 0), iota((16, 128), 0)
     has_right, has_left = gx < ngx - 1, gx > 0
     lane = iota((1, 8, 128), 2)
+
+    table_e = [jnp.full((16, 128), eps_t[k], F32) for k in range(eps_t.shape[0])]
+    table_s = [jnp.full((16, 128), scr_t[k], F32) for k in range(eps_t.shape[0])]
 
     def look(i):
         c = codes[pl.ds(i, 16, stride=16), :]
         e = jnp.zeros((16, 128), F32)
         s = jnp.zeros((16, 128), F32)
         for k in range(eps_t.shape[0]):
-            e = jnp.where(c == k, eps_t[k], e)
-            s = jnp.where(c == k, scr_t[k], s)
+            e = jnp.where(c == k, table_e[k], e)
+            s = jnp.where(c == k, table_s[k], s)
         l0.E[i + 1, 0:16, :] = e
         l0.S[i, 0:16, :] = s
         l0.F[i, 0:16, :] = charge[pl.ds(i, 16, stride=16), :]
 
-    loop(16, look)
+    for copy in inputs:
+        copy.wait()
+    unrolled(16, look)
 
     xs[0, :, 0:2, :] = l0.E[1:17, 14:16, :]
     xs[0, :, 2:3, :] = l0.S[:, 15:16, :]
@@ -307,7 +322,7 @@
         return jnp.where((lane & 1) == 0, v[:, 0], v[:, 1])
 
     es[0, gz, 0:4] = pack2(halve(l0.E[1:17, 0:16, :], 0, tmp))
-    es[0, gz, 4:8] = pack2(halve(l0.S[:, 0:16, :], 0, tmp))
+    es[0, gz, 4:8] = pack2(halve(l0.S[:, 0:16, :], 0, tmp, 8))
 
     def to_lines(buf, ss, rs, act):
         mine = buf.at[0, gz]
@@ -330,7 +345,16 @@
         loop(ngz, lambda k: get(1, k))
         loop(ngz, lambda k: get(2, k))
 
-    to_lines(es, s_es, r_es, lambda c: c.start())
+    def es_lines(act):
+        loop(ngz - 1, lambda k: act(remote(es.at[0, gz], es.at[0, gz], s_es.at[0, k + 1], r_es.at[0, gz], gx, gz_at(k + 1))))
+
+    def es_planes():
+        return [
+            remote(es.at[0], es.at[2], s_es.at[2, 0], r_es.at[2, 0], gx_at(1), gz),
+            remote(es.at[0], es.at[1], s_es.at[1, 0], r_es.at[1, 0], gx_at(-1), gz),
+        ]
+
+    es_lines(lambda c: c.start())
 
     for copy in r1_copies():
         copy.wait_recv()
@@ -421,7 +445,14 @@
 
     gather(red, s_red, r_red, lambda c: c.start())
 
-    from_lines(es, s_es, r_es)
+    def es_line_in(k):
+        p = gz_at(k + 1)
+        remote(es.at[0, gz], es.at[0, p], s_es.at[0, k + 1], r_es.at[0, p], gx, p).wait_recv()
+
+    loop(ngz - 1, es_line_in)
+    for copy in es_planes():
+        copy.start()
+
     mask1 = jnp.where(row24 < 8, 1.0, jnp.where(row24 < 16, jnp.where(has_right, 1.0, 0.0), jnp.where(has_left, 1.0, 0.0)))
     mask2 = jnp.where(
         row16 < 4,
@@ -437,33 +468,30 @@
 
     here = (None, has_right, has_left)
 
-    def place(buf, start, dst, offset, outside):
-        for slot in range(3):
-
-            def body(p, slot=slot):
+    def place(buf, start, dst, offset, outside, slots):
+        for slot in slots:
+            for p in range(ngz):
                 v = unpack2(buf[slot, p, start : start + 4])
                 if slot:
                     v = jnp.where(here[slot], v, outside)
-                dst[pl.ds(p * 8 + offset, 8), slot * 8 : slot * 8 + 8, :] = v
-
-            loop(ngz, body)
-
-    place(es, 0, l1.E, 1, 0.0)
-    place(es, 4, l1.S, 0, 1.0)
+                dst[p * 8 + offset : p * 8 + offset + 8, slot * 8 : slot * 8 + 8, :] = v
+
+    place(es, 0, l1.E, 1, 0.0, (0,))
+    place(es, 4, l1.S, 0, 1.0, (0,))
 
     def coarsen(src, offset, fine, coarse, dst, dst_offset, split):
         n = fine.n
 
         def body(i):
-            v = halve(src[pl.ds(i * n + offset, n)], fine.index, tmp)
-            at = pl.ds(i * (n // 2) + dst_offset, n // 2)
+            v = halve(src[i * n + offset : (i + 1) * n + offset], fine.index, tmp, i * (n // 2))
+            at = slice(i * (n // 2) + dst_offset, (i + 1) * (n // 2) + dst_offset)
             if split:
                 dst[at, 0:8, :] = v[:, 0:8]
                 dst[at, 12:16, :] = v[:, 8:12]
             else:
                 dst[at] = v
 
-        loop(fine.Z // n, body)
+        unrolled(fine.Z // n, body)
 
     def filler(ref, value):
         ref[:, 8:12, :] = jnp.full((ref.shape[0], 4, 128), value, F32)
@@ -471,14 +499,12 @@
     filler(l2.E, 0.0)
     filler(l2.S, 1.0)
     filler(l2.F, 0.0)
-    coarsen(l1.E, 1, l1, l2, l2.E, 1, True)
-    coarsen(l1.S, 0, l1, l2, l2.S, 0, True)
 
     lane3 = iota((4, 2, 128), 2)
 
     def pack4(src, offset, buf, first):
         for i in range(2):
-            v = halve(src[i * 16 + offset : i * 16 + offset + 16], 2, tmp)[:, 0:2]
+            v = halve(src[i * 16 + offset : i * 16 + offset + 16], 2, tmp, i * 8)[:, 0:2]
             tmp[i * 8 : i * 8 + 8, 32:34, :] = v
         v = tmp[0:16, 32:34, :].reshape(4, 4, 2, 128)
         k = (lane3 >> 1) & 3
@@ -486,9 +512,6 @@
         for zz in range(4):
             buf[gx, first + zz * 2 : first + zz * 2 + 2, :] = v[zz]
 
-    pack4(l2.E, 1, es3, 0)
-    pack4(l2.S, 0, es3, 8)
-
     def spread(buf, ss, rs, act):
         loop(ngx - 1, lambda k: act(remote(buf.at[gx], buf.at[gx], ss.at[k + 1], rs.at[gx], gx_at(k + 1), gz)))
 
@@ -498,8 +521,6 @@
             remote(buf.at[gx], buf.at[p], ss.at[k], rs.at[p], p, gz).wait_recv()
 
         loop(ngx - 1, lambda k: get(k + 1))
-
-    spread(es3, s_e3, r_e3, lambda c: c.start())
 
     gathered(red, s_red, r_red)
 
@@ -537,10 +558,19 @@
         z0 = i * 4
         l0.R[pl.ds(z0, 4)] = (1.0 - OMEGA) * l0.F[pl.ds(z0, 4)] + lateral(l0, l0.U[pl.ds(z0, 4)], z0, 4)
 
-    loop(4, first_residual)
+    unrolled(4, first_residual)
     f1[0, gz] = pack2(halve(l0.R[:, 0:16, :], 0, tmp))
     to_lines(f1, s_f1, r_f1, lambda c: c.start())
 
+    for copy in es_planes():
+        copy.wait_recv()
+    place(es, 0, l1.E, 1, 0.0, (1, 2))
+    place(es, 4, l1.S, 0, 1.0, (1, 2))
+    coarsen(l1.E, 1, l1, l2, l2.E, 1, True)
+    coarsen(l1.S, 0, l1, l2, l2.S, 0, True)
+    pack4(l2.E, 1, es3, 0)
+    pack4(l2.S, 0, es3, 8)
+    spread(es3, s_e3, r_e3, lambda c: c.start())
     prepare(l1)
     prepare(l2)
 
@@ -562,7 +592,7 @@
                         dst[offset + zz * 4 + k1 * 2 + k0, pl.ds(xp, ngx, stride=2), :] = v2
 
     from_lines(f1, s_f1, r_f1)
-    place(f1, 0, l1.F, 0, 0.0)
+    place(f1, 0, l1.F, 0, 0.0, (0, 1, 2))
     pre(l1)
     coarsen(l1.R, 0, l1, l2, l2.F, 0, True)
     pre(l2)
@@ -586,22 +616,30 @@
         coarsen(fine.R, 0, fine, coarse, coarse.F, 0, False)
     coarsest(l6)
     for fine, coarse in zip(deep[-2::-1], deep[:0:-1]):
-        loop(coarse.Z, lambda z, fine=fine, coarse=coarse: spread_rows(fine.V, 2 * z + 1, coarse.C[z + 1], ((0, coarse.X, 0),)))
+        unrolled(coarse.Z, lambda z, fine=fine, coarse=coarse: spread_rows(fine.V, 2 * z + 1, coarse.C[z + 1], ((0, coarse.X, 0),)))
         post(fine)
 
+    tiles = ngx // 4
+    first = gx // 4
+    shift = lax.rem(24 - 2 * lax.rem(gx, 4), 24)
+
+    def tile_at(z, k):
+        return l3.C[z, pl.ds(pl.multiple_of(lax.rem(first + (k + tiles), tiles) * 8, 8), 8), :]
+
+    right_rows, left_rows = (iota((4, 128), 0) < 2) | has_right, has_left
+
     def down3(z):
-        c = pltpu.roll(l3.C[z + 1], lax.rem(2 * (ngx - gx), 2 * ngx), 0)
-        spread_rows(l2.V, 2 * z + 1, c, ((0, 4, 0), (62, 2, 12)))
+        c = jnp.concatenate([tile_at(z + 1, 0), tile_at(z + 1, 1), tile_at(z + 1, -1)], axis=0)
+        c = pltpu.roll(c, shift, 0)
+        for k in range(2):
+            for j in range(2):
+                l2.V[2 * z + 1 + k, pl.ds(j, 4, stride=2), :] = jnp.where(right_rows, c[0:4], 0.0)
+                l2.V[2 * z + 1 + k, pl.ds(12 + j, 2, stride=2), :] = jnp.where(left_rows, c[22:24], 0.0)
 
     filler(l2.V, 0.0)
-    loop(l3.Z, down3)
-
-    def clear(i):
-        l2.V[i + 1] = jnp.where(mask2 > 0, l2.V[i + 1], 0.0)
-
-    loop(l2.Z, clear)
+    unrolled(l3.Z, down3)
     post(l2)
-    loop(l2.Z, lambda z: spread_rows(l1.V, 2 * z + 1, l2.C[z + 1], ((0, 4, 0), (4, 4, 8), (12, 4, 16))))
+    unrolled(l2.Z, lambda z: spread_rows(l1.V, 2 * z + 1, l2.C[z + 1], ((0, 4, 0), (4, 4, 8), (12, 4, 16))))
     post(l1)
     l1.C[0] = jnp.zeros((24, 128), F32)
     l1.C[l1.Z + 1] = jnp.zeros((24, 128), F32)
@@ -622,7 +660,7 @@
         around = lateral(l0, v, z0, 4) + l0.WZ[pl.ds(z0, 4)] * l0.V[pl.ds(z0, 4)] + l0.WZ[pl.ds(z0 + 1, 4)] * l0.V[pl.ds(z0 + 2, 4)]
         l0.F[pl.ds(z0, 4)] = l0.R[pl.ds(z0, 4)] - (l0.D[pl.ds(z0, 4)] * v - around)
 
-    loop(4, second_residual)
+    unrolled(4, second_residual)
     inner(l0.F)
     post_red[gz, 0:16, :] = (l0.F[15] + tail * l0.Y[14])[0:16]
     post_red[gz, 16:32, :] = (lead * l0.Y[0])[0:16]
@@ -652,7 +690,9 @@
 
     for copy in r1_copies():
         copy.wait_send()
-    to_lines(es, s_es, r_es, lambda c: c.wait_send())
+    es_lines(lambda c: c.wait_send())
+    for copy in es_planes():
+        copy.wait_send()
     to_lines(f1, s_f1, r_f1, lambda c: c.wait_send())
     gather(red, s_red, r_red, lambda c: c.wait_send())
     gather(post_red, s_post, r_post, lambda c: c.wait_send())
@@ -680,7 +720,10 @@
             scratch += Level.scratch(Z, X)
         vm = lambda *shape: pltpu.VMEM(shape, F32)
         scratch += [
-            vm(16, 64, 128),
+            vm(64, 64, 128),
+            pltpu.VMEM((nx * nz, ny), jnp.int32),
+            vm(nx * nz, ny),
+            pltpu.SemaphoreType.DMA((2,)),
             vm(2, 16, 4, 128),
             vm(2, 16, 4, 128),
             vm(2, 16, 128),
@@ -705,8 +748,8 @@
             lambda *refs: kernel(ngx, ngz, *refs),
             out_shape=jax.ShapeDtypeStruct((nx * nz, ny), F32),
             in_specs=[
-                pl.BlockSpec(memory_space=pltpu.VMEM),
-                pl.BlockSpec(memory_space=pltpu.VMEM),
+                pl.BlockSpec(memory_space=pl.ANY),
+                pl.BlockSpec(memory_space=pl.ANY),
                 pl.BlockSpec(memory_space=pltpu.SMEM),
                 pl.BlockSpec(memory_space=pltpu.SMEM),
             ],

time: 82.1 us -> 65.3 us (0.80)
  Pallas kernels: 80.5 us -> 63.6 us
    pallas_call x1, Pallas kernels: 80.5 us -> 63.6 us  [per_device(): pl.pallas_call(lambda *refs: kernel(ngx, ngz, *refs), out_shape=jax.Shape...]
where the time goes in v1:
time: 65.3 us; the launch traced here: 65.2 us
  Pallas kernels  63.6 us (97%)
  local copies, waits for them, and re-layouts  1.57 us (2%)
    pallas_call x1, Pallas kernels, per_device(): pl.pallas_call(lambda *refs: kernel(ngx, ngz, *refs), out_shape=jax.Shape...  63.6 us
    unnamed x1, local copies, waits for them, and re-layouts  1.57 us

profile of v1, /device:TPU:1, one launch (start us, length us, event | category | flops | bytes accessed | tf_op | source)
XLA Modules:
  0.0 65.2 jit_solution(13382701662066110563)
XLA Ops:
  0.0 63.6 %vcycle.1 = f32[256,128]{1,0:T(8,128)} custom-call(s32[256,128]{1,0:T(8,128)} %bitcast.4, f32[256,128]{1,0:T(8,128)} %bitcast.5, f32[8]{0:T(128)} %refs_2_.1, f32[8]{0:T(128)} %refs_3_.1), custom_call_target="tpu_custom_call" | custom-call | tf_op jit(solution)/shard_map/vcycle/pallas_call | solution.py:747
  63.6 1.6 %copy.6 = f32[16,16,128]{2,1,0:T(8,128)} copy(f32[16,16,128]{2,1,0:T(8,128)} %bitcast.3) | data formatting | bytes 262144

commit v2 on v1

--- a/solution.py
+++ b/solution.py
@@ -238,8 +238,8 @@
     l4 = Level(4, take(16), True, 4)
     l5 = Level(5, take(16), True, 4)
     l6 = Level(6, take(16), True, 2)
-    (tmp, codes, charge, s_in, xs, xr, zs, zr, ds, dr, es, f1, red, post_red, ub, rm, ra, av, bv, es3, f3) = take(21)
-    (s_r1, r_r1, s_es, r_es, s_f1, r_f1, s_red, r_red, s_post, r_post, s_e3, r_e3, s_f3, r_f3) = take(14)
+    (tmp, codes, charge, s_in, xs, xr, zs, zr, ds, dr, es, f1, red, post_red, ub, rm, ra, av, bv, es3, f3, fh, fr, f2, f2r) = take(25)
+    (s_r1, r_r1, s_es, r_es, s_f1, r_f1, s_red, r_red, s_post, r_post, s_e3, r_e3, s_f3, r_f3, s_f2, r_f2) = take(16)
 
     gx, gz = lax.axis_index("gx"), lax.axis_index("gz")
 
@@ -324,26 +324,22 @@
     es[0, gz, 0:4] = pack2(halve(l0.E[1:17, 0:16, :], 0, tmp))
     es[0, gz, 4:8] = pack2(halve(l0.S[:, 0:16, :], 0, tmp, 8))
 
-    def to_lines(buf, ss, rs, act):
-        mine = buf.at[0, gz]
-
-        def go(slot, k, tx):
-            act(remote(mine, buf.at[slot, gz], ss.at[slot, k], rs.at[slot, gz], tx, gz_at(k)))
-
-        loop(ngz - 1, lambda k: go(0, k + 1, gx))
-        loop(ngz, lambda k: go(2, k, gx_at(1)))
-        loop(ngz, lambda k: go(1, k, gx_at(-1)))
-
-    def from_lines(buf, ss, rs):
-        mine = buf.at[0, gz]
-
-        def get(slot, k):
+    def f1_copies(act):
+        def go(slot, k, src, dst, tx):
+            act(remote(src, dst, s_f1.at[slot, k], r_f1.at[slot, gz], tx, gz_at(k)))
+
+        loop(ngz - 1, lambda k: go(0, k + 1, f1.at[gz], f1.at[gz], gx))
+        loop(ngz, lambda k: go(1, k, fh.at[0], fr.at[0, gz], gx_at(1)))
+        loop(ngz, lambda k: go(2, k, fh.at[1], fr.at[1, gz], gx_at(-1)))
+
+    def f1_arrive():
+        def get(slot, dst, k):
             p = gz_at(k)
-            remote(mine, buf.at[slot, p], ss.at[slot, k], rs.at[slot, p], gx, gz_at(1)).wait_recv()
-
-        loop(ngz - 1, lambda k: get(0, k + 1))
-        loop(ngz, lambda k: get(1, k))
-        loop(ngz, lambda k: get(2, k))
+            remote(dst, dst, s_f1.at[slot, k], r_f1.at[slot, p], gx, gz_at(1)).wait_recv()
+
+        loop(ngz - 1, lambda k: get(0, f1.at[gz], k + 1))
+        loop(ngz, lambda k: get(1, fr.at[0, gz], k))
+        loop(ngz, lambda k: get(2, fr.at[1, gz], k))
 
     def es_lines(act):
         loop(ngz - 1, lambda k: act(remote(es.at[0, gz], es.at[0, gz], s_es.at[0, k + 1], r_es.at[0, gz], gx, gz_at(k + 1))))
@@ -559,8 +555,12 @@
         l0.R[pl.ds(z0, 4)] = (1.0 - OMEGA) * l0.F[pl.ds(z0, 4)] + lateral(l0, l0.U[pl.ds(z0, 4)], z0, 4)
 
     unrolled(4, first_residual)
-    f1[0, gz] = pack2(halve(l0.R[:, 0:16, :], 0, tmp))
-    to_lines(f1, s_f1, r_f1, lambda c: c.start())
+    packed = pack2(halve(l0.R[:, 0:16, :], 0, tmp))
+    f1[gz] = packed
+    for zz in range(4):
+        fh[0, zz * 4 : zz * 4 + 4, :] = packed[zz, 4:8]
+        fh[1, zz * 4 : zz * 4 + 4, :] = packed[zz, 0:4]
+    f1_copies(lambda c: c.start())
 
     for copy in es_planes():
         copy.wait_recv()
@@ -591,13 +591,36 @@
                         v2 = jnp.where(((lane32 >> 2) & 1) == k1, v1, w1)
                         dst[offset + zz * 4 + k1 * 2 + k0, pl.ds(xp, ngx, stride=2), :] = v2
 
-    from_lines(f1, s_f1, r_f1)
-    place(f1, 0, l1.F, 0, 0.0, (0, 1, 2))
+    l1.F[:, 8:24, :] = jnp.zeros((l1.Z, 16, 128), F32)
+    lane16 = iota((16, 128), 1)
+    f1_arrive()
+    for p in range(ngz):
+        l1.F[p * 8 : p * 8 + 8, 0:8, :] = unpack2(f1[p])
+        for side, present, row in ((0, has_left, 20), (1, has_right, 8)):
+            v = jnp.where(present, fr[side, p], 0.0)
+            both = (jnp.where((lane16 & 1) == 0, v, roll(v, 1, 1)), jnp.where((lane16 & 1) == 1, v, roll(v, -1, 1)))
+            for zz in range(4):
+                for k in range(2):
+                    l1.F[p * 8 + zz * 2 + k, row : row + 4, :] = both[k][zz * 4 : zz * 4 + 4]
     pre(l1)
     coarsen(l1.R, 0, l1, l2, l2.F, 0, True)
     pre(l2)
     pack4(l2.R, 0, f3, 0)
     spread(f3, s_f3, r_f3, lambda c: c.start())
+
+    lane8 = iota((8, 8, 128), 2)
+    v = l2.F[:, 0:8, :].reshape(8, 4, 8, 128)
+    k = lane8 & 3
+    f2[...] = jnp.where(k == 0, v[:, 0], jnp.where(k == 1, v[:, 1], jnp.where(k == 2, v[:, 2], v[:, 3])))
+
+    def f2_copies():
+        return [
+            remote(f2, f2r.at[0], s_f2.at[0], r_f2.at[0], gx_at(1), gz),
+            remote(f2, f2r.at[1], s_f2.at[1], r_f2.at[1], gx_at(-1), gz),
+        ]
+
+    for copy in f2_copies():
+        copy.start()
 
     collected(es3, s_e3, r_e3)
     place4(es3, 16, 0, l3.E, 1)
@@ -608,6 +631,24 @@
         coarsen(fine.S, 0, fine, coarse, coarse.S, 0, False)
     for lev in deep:
         prepare(lev)
+
+    for copy in f2_copies():
+        copy.wait_recv()
+
+    def swap8(v, s):
+        return jnp.where((lane8 & s) == 0, roll(v, -s, 2), roll(v, s, 2))
+
+    for side, present, source, row in ((0, has_left, 2, 14), (1, has_right, 1, 5)):
+        v = jnp.where(present, f2r[side], 0.0)
+        w = swap8(v, 1)
+        for k0 in range(2):
+            v1 = jnp.where((lane8 & 1) == k0, v, w)
+            w1 = swap8(v1, 2)
+            for k1 in range(2):
+                v2 = jnp.where(((lane8 >> 1) & 1) == k1, v1, w1)
+                for zz in range(8):
+                    l2.F[zz * 4 + k1 * 2 + k0, row : row + 1, :] = v2[zz, source : source + 1]
+    pre(l2)
 
     collected(f3, s_f3, r_f3)
     place4(f3, 8, 0, l3.F, 0)
@@ -693,7 +734,9 @@
     es_lines(lambda c: c.wait_send())
     for copy in es_planes():
         copy.wait_send()
-    to_lines(f1, s_f1, r_f1, lambda c: c.wait_send())
+    f1_copies(lambda c: c.wait_send())
+    for copy in f2_copies():
+        copy.wait_send()
     gather(red, s_red, r_red, lambda c: c.wait_send())
     gather(post_red, s_post, r_post, lambda c: c.wait_send())
     spread(es3, s_e3, r_e3, lambda c: c.wait_send())
@@ -731,7 +774,7 @@
             vm(4, 8, 128),
             vm(4, 8, 128),
             vm(3, ngz, 8, 8, 128),
-            vm(3, ngz, 4, 8, 128),
+            vm(ngz, 4, 8, 128),
             vm(ngz, 96, 128),
             vm(ngz, 32, 128),
             vm(ngz + 1, 24, 128),
@@ -741,8 +784,12 @@
             vm(16, 24, 128),
             vm(ngx, 16, 128),
             vm(ngx, 8, 128),
+            vm(2, 16, 128),
+            vm(2, ngz, 16, 128),
+            vm(8, 8, 128),
+            vm(2, 8, 8, 128),
         ]
-        for shape in ((8,), (3, ngz), (3, ngz), (ngz,), (ngz,), (ngx,), (ngx,)):
+        for shape in ((8,), (3, ngz), (3, ngz), (ngz,), (ngz,), (ngx,), (ngx,), (2,)):
             scratch += [pltpu.SemaphoreType.DMA(shape)] * 2
         result = pl.pallas_call(
             lambda *refs: kernel(ngx, ngz, *refs),

time: 65.3 us -> 61.7 us (0.945)
  Pallas kernels: 63.6 us -> 60 us
    pallas_call x1, Pallas kernels: 63.6 us -> 60 us  [per_device(): pl.pallas_call(lambda *refs: kernel(ngx, ngz, *refs), out_shape=jax.Shape...]
where the time goes in v2:
time: 61.7 us; the launch traced here: 61.6 us
  Pallas kernels  60 us (97%)
  local copies, waits for them, and re-layouts  1.57 us (3%)
    pallas_call x1, Pallas kernels, per_device(): pl.pallas_call(lambda *refs: kernel(ngx, ngz, *refs), out_shape=jax.Shape...  60 us
    unnamed x1, local copies, waits for them, and re-layouts  1.57 us

profile of v2, /device:TPU:1, one launch (start us, length us, event | category | flops | bytes accessed | tf_op | source)
XLA Modules:
  0.0 61.6 jit_solution(892935417876593064)
XLA Ops:
  0.0 60.0 %vcycle.1 = f32[256,128]{1,0:T(8,128)} custom-call(s32[256,128]{1,0:T(8,128)} %bitcast.4, f32[256,128]{1,0:T(8,128)} %bitcast.5, f32[8]{0:T(128)} %refs_2_.1, f32[8]{0:T(128)} %refs_3_.1), custom_call_target="tpu_custom_call" | custom-call | tf_op jit(solution)/shard_map/vcycle/pallas_call | solution.py:794
  60.0 1.6 %copy.6 = f32[16,16,128]{2,1,0:T(8,128)} copy(f32[16,16,128]{2,1,0:T(8,128)} %bitcast.3) | data formatting | bytes 262144

commit v3 on v2

--- a/solution.py
+++ b/solution.py
@@ -10,6 +10,7 @@
 LAST = 6
 F32 = jnp.float32
 MESH = pl.DeviceIdType.MESH
+FAR_FIRST = (4, 3, 5, 2, 6, 1, 7)
 
 
 def iota(shape, dim):
@@ -194,24 +195,33 @@
 
 def coarsest(lev):
     Z = lev.Z
-
-    def first(z, x):
-        lev.U[z] = OMEGA * x
-
-    def again(z, x):
-        lev.U[z] = (1.0 - OMEGA) * lev.U[z] + OMEGA * x
-
-    def last(z, x):
-        lev.C[z + 1] = (1.0 - OMEGA) * lev.U[z] + OMEGA * x
-
-    sweep(lev, lev.F, first)
-
-    def once(finish):
-        lev.R[...] = lev.F[...] + lateral(lev, lev.U[...], 0, Z)
-        sweep(lev, lev.R, finish)
-
-    loop(SWEEPS - 2, lambda i: once(again))
-    once(last)
+    sh = 2 ** lev.index
+    f = [lev.F[z] for z in range(Z)]
+    a = [lev.A[z] for z in range(Z + 1)]
+    m = [lev.M[z] for z in range(Z)]
+    w = [(lev.WXM[z], lev.WXP[z], lev.WYM[z], lev.WYP[z]) for z in range(Z)]
+
+    def solved(r):
+        y = [r[0]]
+        for z in range(1, Z):
+            y.append(r[z] + a[z] * y[-1])
+        x = [None] * Z
+        x[Z - 1] = m[Z - 1] * y[Z - 1]
+        for z in range(Z - 2, -1, -1):
+            x[z] = m[z] * y[z] + a[z + 1] * x[z + 1]
+        return x
+
+    u = [OMEGA * x for x in solved(f)]
+    for _ in range(SWEEPS - 1):
+        r = []
+        for z in range(Z):
+            xm, xp, ym, yp = w[z]
+            side = xm * roll(u[z], 1, 0) + xp * roll(u[z], -1, 0)
+            r.append(f[z] + (side + (ym * roll(u[z], sh, 1) + yp * roll(u[z], -sh, 1))))
+        x = solved(r)
+        u = [(1.0 - OMEGA) * u[z] + OMEGA * x[z] for z in range(Z)]
+    for z in range(Z):
+        lev.C[z + 1] = u[z]
 
 
 def spread_rows(dst, z, c, rows):
@@ -238,7 +248,7 @@
     l4 = Level(4, take(16), True, 4)
     l5 = Level(5, take(16), True, 4)
     l6 = Level(6, take(16), True, 2)
-    (tmp, codes, charge, s_in, xs, xr, zs, zr, ds, dr, es, f1, red, post_red, ub, rm, ra, av, bv, es3, f3, fh, fr, f2, f2r) = take(25)
+    (tmp, codes, charge, s_in, xs, xr, zs, zr, ds, dr, es, f1, red, post_red, ub, rm, ra, av, bv, es3, f3, fh, fr, f2, f2r, ps, rb, pivots, mid) = take(29)
     (s_r1, r_r1, s_es, r_es, s_f1, r_f1, s_red, r_red, s_post, r_post, s_e3, r_e3, s_f3, r_f3, s_f2, r_f2) = take(16)
 
     gx, gz = lax.axis_index("gx"), lax.axis_index("gz")
@@ -301,6 +311,13 @@
     ds[2] = l0.E[1, 8:16, :]
     ds[3] = l0.E[1, 0:8, :]
 
+    def pack2(v):
+        v = v.reshape(4, 2, 8, 128)
+        return jnp.where((lane & 1) == 0, v[:, 0], v[:, 1])
+
+    es[0, gz, 0:4] = pack2(halve(l0.E[1:17, 0:16, :], 0, tmp))
+    es[0, gz, 4:8] = pack2(halve(l0.S[:, 0:16, :], 0, tmp, 8))
+
     def r1_copies():
         return [
             remote(xs.at[0], xr.at[0], s_r1.at[0], r_r1.at[0], gx_at(1), gz),
@@ -317,20 +334,15 @@
     for copy in r1_copies():
         copy.start()
 
-    def pack2(v):
-        v = v.reshape(4, 2, 8, 128)
-        return jnp.where((lane & 1) == 0, v[:, 0], v[:, 1])
-
-    es[0, gz, 0:4] = pack2(halve(l0.E[1:17, 0:16, :], 0, tmp))
-    es[0, gz, 4:8] = pack2(halve(l0.S[:, 0:16, :], 0, tmp, 8))
-
     def f1_copies(act):
         def go(slot, k, src, dst, tx):
             act(remote(src, dst, s_f1.at[slot, k], r_f1.at[slot, gz], tx, gz_at(k)))
 
-        loop(ngz - 1, lambda k: go(0, k + 1, f1.at[gz], f1.at[gz], gx))
-        loop(ngz, lambda k: go(1, k, fh.at[0], fr.at[0, gz], gx_at(1)))
-        loop(ngz, lambda k: go(2, k, fh.at[1], fr.at[1, gz], gx_at(-1)))
+        for k in (4, 3, 5, 2, 6, 1, 7, 0):
+            if k:
+                go(0, k, f1.at[gz], f1.at[gz], gx)
+            go(1, k, fh.at[0], fr.at[0, gz], gx_at(1))
+            go(2, k, fh.at[1], fr.at[1, gz], gx_at(-1))
 
     def f1_arrive():
         def get(slot, dst, k):
@@ -342,7 +354,8 @@
         loop(ngz, lambda k: get(2, fr.at[1, gz], k))
 
     def es_lines(act):
-        loop(ngz - 1, lambda k: act(remote(es.at[0, gz], es.at[0, gz], s_es.at[0, k + 1], r_es.at[0, gz], gx, gz_at(k + 1))))
+        for k in FAR_FIRST:
+            act(remote(es.at[0, gz], es.at[0, gz], s_es.at[0, k], r_es.at[0, gz], gx, gz_at(k)))
 
     def es_planes():
         return [
@@ -430,7 +443,13 @@
     put(4, lead * l0.Y[0])
 
     def gather(buf, ss, rs, act):
-        loop(ngz - 1, lambda k: act(remote(buf.at[gz], buf.at[gz], ss.at[k + 1], rs.at[gz], gx, gz_at(k + 1))))
+        for k in FAR_FIRST:
+            act(remote(buf.at[gz], buf.at[gz], ss.at[k], rs.at[gz], gx, gz_at(k)))
+
+    def post_copies(act):
+        for k in FAR_FIRST:
+            side = lax.div(gz + k, ngz)
+            act(remote(ps.at[side], post_red.at[gz], s_post.at[k], r_post.at[gz], gx, gz_at(k)))
 
     def gathered(buf, ss, rs):
         def get(k):
@@ -562,6 +581,22 @@
         fh[1, zz * 4 : zz * 4 + 4, :] = packed[zz, 0:4]
     f1_copies(lambda c: c.start())
 
+    q = got(ngz - 1, 1)[0:16]
+    pivots[ngz - 1] = q
+    for p in range(ngz - 1, 0, -1):
+        c = got(p, 0)[0:16]
+        b = c * (1.0 / q)
+        rb[p] = b
+        q = got(p - 1, 1)[0:16] - got(p, 2)[0:16] - c * b
+        pivots[p - 1] = q
+    rb[0] = jnp.zeros((16, 128), F32)
+    c = jnp.where(above, red[gz, 0:16, :], 0.0)
+    left = rm[jnp.maximum(gz - 1, 0), 0:16, :]
+    mid[0] = left
+    mid[1] = c * left
+    mid[2] = 1.0 / (pivots[gz] - c * c * left)
+    mid[3] = c
+
     for copy in es_planes():
         copy.wait_recv()
     place(es, 0, l1.E, 1, 0.0, (1, 2))
@@ -703,31 +738,30 @@
 
     unrolled(4, second_residual)
     inner(l0.F)
-    post_red[gz, 0:16, :] = (l0.F[15] + tail * l0.Y[14])[0:16]
-    post_red[gz, 16:32, :] = (lead * l0.Y[0])[0:16]
-    gather(post_red, s_post, r_post, lambda c: c.start())
+    end_row, first_row = (l0.F[15] + tail * l0.Y[14])[0:16], (lead * l0.Y[0])[0:16]
+    ps[0] = end_row + jnp.where(above, ra[gz, 0:16, :], 0.0) * first_row
+    ps[1] = first_row + rb[gz] * end_row
+    post_red[gz] = jnp.zeros((16, 128), F32)
+    post_copies(lambda c: c.start())
+    for z in range(16):
+        l0.U[z, 0:16, :] = l0.U[z, 0:16, :] + l0.V[z + 1, 0:16, :]
     gathered(post_red, s_post, r_post)
-    y = None
-    for p in range(ngz):
-        right = post_red[p, 0:16, :]
-        if p + 1 < ngz:
-            right = right + post_red[p + 1, 16:32, :]
-        if p:
-            right = right + ra[p, 0:16, :] * y
-        y = right
-        ub[p + 1, 0:16, :] = y
-    x = rm[ngz - 1, 0:16, :] * y
-    for p in range(ngz - 1, -1, -1):
-        if p + 1 < ngz:
-            x = rm[p, 0:16, :] * ub[p + 1, 0:16, :] + ra[p + 1, 0:16, :] * x
-        ub[p + 1, 0:16, :] = x
-    before, own = ub[gz, 0:16, :], ub[gz + 1, 0:16, :]
+    tau = jnp.zeros((16, 128), F32)
+    for p in range(ngz - 1):
+        took = post_red[p] if p == 0 else post_red[p] + ra[p, 0:16, :] * tau
+        tau = jnp.where(p < gz, took, tau)
+    sigma = jnp.zeros((16, 128), F32)
+    for p in range(ngz - 1, 0, -1):
+        sigma = jnp.where(p > gz, post_red[p] + rb[p] * sigma, sigma)
+    b1 = first_row + tau
+    own = mid[2] * (end_row + sigma + mid[1] * b1)
+    before = mid[0] * (b1 + mid[3] * own)
     for z in range(16):
         if z < 15:
             x = l0.Y[z, 0:16, :] + av[z, 0:16, :] * before + bv[z, 0:16, :] * own
         else:
             x = own
-        out[pl.ds(z, 16, stride=16), :] = l0.U[z, 0:16, :] + l0.V[z + 1, 0:16, :] + OMEGA * x
+        out[pl.ds(z, 16, stride=16), :] = l0.U[z, 0:16, :] + OMEGA * x
 
     for copy in r1_copies():
         copy.wait_send()
@@ -738,7 +772,7 @@
     for copy in f2_copies():
         copy.wait_send()
     gather(red, s_red, r_red, lambda c: c.wait_send())
-    gather(post_red, s_post, r_post, lambda c: c.wait_send())
+    post_copies(lambda c: c.wait_send())
     spread(es3, s_e3, r_e3, lambda c: c.wait_send())
     spread(f3, s_f3, r_f3, lambda c: c.wait_send())
 
@@ -776,7 +810,7 @@
             vm(3, ngz, 8, 8, 128),
             vm(ngz, 4, 8, 128),
             vm(ngz, 96, 128),
-            vm(ngz, 32, 128),
+            vm(ngz, 16, 128),
             vm(ngz + 1, 24, 128),
             vm(ngz, 18, 128),
             vm(ngz, 18, 128),
@@ -788,6 +822,10 @@
             vm(2, ngz, 16, 128),
             vm(8, 8, 128),
             vm(2, 8, 8, 128),
+            vm(2, 16, 128),
+            vm(ngz, 16, 128),
+            vm(ngz, 16, 128),
+            vm(4, 16, 128),
         ]
         for shape in ((8,), (3, ngz), (3, ngz), (ngz,), (ngz,), (ngx,), (ngx,), (2,)):
             scratch += [pltpu.SemaphoreType.DMA(shape)] * 2
@@ -802,7 +840,7 @@
             ],
             out_specs=pl.BlockSpec(memory_space=pltpu.VMEM),
             scratch_shapes=scratch,
-            compiler_params=pltpu.CompilerParams(collective_id=0, has_side_effects=True, vmem_limit_bytes=56 << 20),
+            compiler_params=pltpu.CompilerParams(collective_id=0, has_side_effects=True, vmem_limit_bytes=55040 << 10),
             name="vcycle",
         )(codes.reshape(nx * nz, ny), charge.reshape(nx * nz, ny), eps_table, screen_table)
         return result.reshape(nx, nz, ny)

time: 61.7 us -> 58.3 us (0.945); the launches traced: 61.6 us -> 57.4 us
  Pallas kernels: 60 us -> 56.1 us
    pallas_call x1, Pallas kernels: 60 us -> 56.1 us  [per_device(): pl.pallas_call(lambda *refs: kernel(ngx, ngz, *refs), out_shape=jax.Shape...]
    unnamed x1 -> x5, local copies, waits for them, and re-layouts: 1.57 us -> 1.33 us
where the time goes in v3:
time: 58.3 us; the launch traced here: 57.4 us
  Pallas kernels  56.1 us (96%)
  local copies, waits for them, and re-layouts  1.33 us (2%)
    pallas_call x1, Pallas kernels, per_device(): pl.pallas_call(lambda *refs: kernel(ngx, ngz, *refs), out_shape=jax.Shape...  56.1 us
    unnamed x5, local copies, waits for them, and re-layouts  1.33 us

profile of v3, /device:TPU:1, one launch (start us, length us, event | category | flops | bytes accessed | tf_op | source)
XLA Modules:
  0.0 57.4 jit_solution(7092673192369448986)
XLA Ops:
  0.0 0.0 copy-start
  0.0 0.0 copy-start.1
  0.0 0.7 %copy-done = f32[8]{0:T(128)S(1)} copy-done((f32[8]{0:T(128)S(1)}, f32[8]{0:T(128)}, u32[]{:S(2)}) %copy-start) | copy-done | bytes 56
  0.7 0.0 copy-done.1
  0.7 56.1 %vcycle.1 = f32[256,128]{1,0:T(8,128)S(1)} custom-call(s32[256,128]{1,0:T(8,128)} %bitcast.4, f32[256,128]{1,0:T(8,128)} %bitcast.5, f32[8]{0:T(128)S(1)} %copy-done, f32[8]{0:T(128)S(1)} %copy-done.1), custom_call_target="tpu_custom_call" | custom-call | tf_op jit(solution)/shard_map/vcycle/pallas_call | solution.py:832
  56.8 0.7 %copy.6 = f32[16,16,128]{2,1,0:T(8,128)} copy(f32[16,16,128]{2,1,0:T(8,128)S(1)} %bitcast.3) | data formatting | bytes 262144
Async XLA Ops:
  0.0 0.7 %copy-start = (f32[8]{0:T(128)S(1)}, f32[8]{0:T(128)}, u32[]{:S(2)}) copy-start(f32[8]{0:T(128)} %refs_2_.1) | copy-start | bytes 100
  0.0 0.7 %copy-start.1 = (f32[8]{0:T(128)S(1)}, f32[8]{0:T(128)}, u32[]{:S(2)}) copy-start(f32[8]{0:T(128)} %refs_3_.1) | copy-start | bytes 100

commit v4 on v3

--- a/solution.py
+++ b/solution.py
@@ -515,20 +515,26 @@
     filler(l2.S, 1.0)
     filler(l2.F, 0.0)
 
-    lane3 = iota((4, 2, 128), 2)
-
-    def pack4(src, offset, buf, first):
+    lane3 = iota((2, 2, 128), 2)
+
+    def pack8(src, offset, buf, first):
         for i in range(2):
             v = halve(src[i * 16 + offset : i * 16 + offset + 16], 2, tmp, i * 8)[:, 0:2]
             tmp[i * 8 : i * 8 + 8, 32:34, :] = v
-        v = tmp[0:16, 32:34, :].reshape(4, 4, 2, 128)
-        k = (lane3 >> 1) & 3
-        v = jnp.where(k == 0, v[:, 0], jnp.where(k == 1, v[:, 1], jnp.where(k == 2, v[:, 2], v[:, 3])))
-        for zz in range(4):
-            buf[gx, first + zz * 2 : first + zz * 2 + 2, :] = v[zz]
+        v = tmp[0:16, 32:34, :].reshape(2, 8, 2, 128)
+        picked = v[:, 7]
+        for k in range(7):
+            picked = jnp.where((lane3 & 7) == k, v[:, k], picked)
+        for zz in range(2):
+            buf[gx, first + zz * 2 : first + zz * 2 + 2, :] = picked[zz]
+
+    core, x4, y4 = lax.rem(gx, 2), lax.rem(lax.div(gx, 2), 4), lax.div(gx, 8)
+    hops = sorted(((dy, dx, dc) for dy in range(4) for dx in range(4) for dc in range(2)), key=lambda t: -(min(t[0], 4 - t[0]) + min(t[1], 4 - t[1]) + 0.5 * t[2]))
+    far_gx = [lax.rem(y4 + dy, 4) * 8 + lax.rem(x4 + dx, 4) * 2 + lax.rem(core + dc, 2) for dy, dx, dc in hops[:-1]]
 
     def spread(buf, ss, rs, act):
-        loop(ngx - 1, lambda k: act(remote(buf.at[gx], buf.at[gx], ss.at[k + 1], rs.at[gx], gx_at(k + 1), gz)))
+        for i, tx in enumerate(far_gx):
+            act(remote(buf.at[gx], buf.at[gx], ss.at[i], rs.at[gx], tx, gz))
 
     def collected(buf, ss, rs):
         def get(k):
@@ -603,8 +609,8 @@
     place(es, 4, l1.S, 0, 1.0, (1, 2))
     coarsen(l1.E, 1, l1, l2, l2.E, 1, True)
     coarsen(l1.S, 0, l1, l2, l2.S, 0, True)
-    pack4(l2.E, 1, es3, 0)
-    pack4(l2.S, 0, es3, 8)
+    pack8(l2.E, 1, es3, 0)
+    pack8(l2.S, 0, es3, 4)
     spread(es3, s_e3, r_e3, lambda c: c.start())
     prepare(l1)
     prepare(l2)
@@ -614,17 +620,19 @@
     def swap(v, s):
         return jnp.where((lane32 & s) == 0, roll(v, -s, 1), roll(v, s, 1))
 
-    def place4(buf, rows, first, dst, offset):
-        for zz in range(4):
+    def place8(buf, first, dst, offset):
+        for zz in range(2):
             for xp in range(2):
-                v = buf[:, first + zz * 2 + xp, :]
-                w = swap(v, 2)
-                for k0 in range(2):
-                    v1 = jnp.where(((lane32 >> 1) & 1) == k0, v, w)
-                    w1 = swap(v1, 4)
-                    for k1 in range(2):
-                        v2 = jnp.where(((lane32 >> 2) & 1) == k1, v1, w1)
-                        dst[offset + zz * 4 + k1 * 2 + k0, pl.ds(xp, ngx, stride=2), :] = v2
+                found = [(buf[:, first + zz * 2 + xp, :], 0)]
+                for bit in (1, 2, 4):
+                    split = []
+                    for v, z in found:
+                        w = swap(v, bit)
+                        low = (lane32 & bit) == 0
+                        split += [(jnp.where(low, v, w), z), (jnp.where(low, w, v), z + bit)]
+                    found = split
+                for v, z in found:
+                    dst[offset + zz * 8 + z, pl.ds(xp, ngx, stride=2), :] = v
 
     l1.F[:, 8:24, :] = jnp.zeros((l1.Z, 16, 128), F32)
     lane16 = iota((16, 128), 1)
@@ -639,10 +647,6 @@
                     l1.F[p * 8 + zz * 2 + k, row : row + 4, :] = both[k][zz * 4 : zz * 4 + 4]
     pre(l1)
     coarsen(l1.R, 0, l1, l2, l2.F, 0, True)
-    pre(l2)
-    pack4(l2.R, 0, f3, 0)
-    spread(f3, s_f3, r_f3, lambda c: c.start())
-
     lane8 = iota((8, 8, 128), 2)
     v = l2.F[:, 0:8, :].reshape(8, 4, 8, 128)
     k = lane8 & 3
@@ -657,9 +661,13 @@
     for copy in f2_copies():
         copy.start()
 
+    pre(l2)
+    pack8(l2.R, 0, f3, 0)
+    spread(f3, s_f3, r_f3, lambda c: c.start())
+
     collected(es3, s_e3, r_e3)
-    place4(es3, 16, 0, l3.E, 1)
-    place4(es3, 16, 8, l3.S, 0)
+    place8(es3, 0, l3.E, 1)
+    place8(es3, 4, l3.S, 0)
     deep = [l3, l4, l5, l6]
     for fine, coarse in zip(deep[:-1], deep[1:]):
         coarsen(fine.E, 1, fine, coarse, coarse.E, 1, False)
@@ -686,7 +694,7 @@
     pre(l2)
 
     collected(f3, s_f3, r_f3)
-    place4(f3, 8, 0, l3.F, 0)
+    place8(f3, 0, l3.F, 0)
     for fine, coarse in zip(deep[:-1], deep[1:]):
         pre(fine)
         coarsen(fine.R, 0, fine, coarse, coarse.F, 0, False)
@@ -809,15 +817,15 @@
             vm(4, 8, 128),
             vm(3, ngz, 8, 8, 128),
             vm(ngz, 4, 8, 128),
-            vm(ngz, 96, 128),
+            vm(ngz, 90, 128),
             vm(ngz, 16, 128),
             vm(ngz + 1, 24, 128),
             vm(ngz, 18, 128),
             vm(ngz, 18, 128),
             vm(16, 24, 128),
             vm(16, 24, 128),
-            vm(ngx, 16, 128),
             vm(ngx, 8, 128),
+            vm(ngx, 4, 128),
             vm(2, 16, 128),
             vm(2, ngz, 16, 128),
             vm(8, 8, 128),

time: 58.3 us -> 56.6 us (0.971); the launches traced: 57.4 us -> 56.5 us
  Pallas kernels: 56.1 us -> 55.2 us
    pallas_call x1, Pallas kernels: 56.1 us -> 55.2 us  [per_device(): pl.pallas_call(lambda *refs: kernel(ngx, ngz, *refs), out_shape=jax.Shape...]
where the time goes in v4:
time: 56.6 us; the launch traced here: 56.5 us
  Pallas kernels  55.2 us (98%)
  local copies, waits for them, and re-layouts  1.33 us (2%)
    pallas_call x1, Pallas kernels, per_device(): pl.pallas_call(lambda *refs: kernel(ngx, ngz, *refs), out_shape=jax.Shape...  55.2 us
    unnamed x5, local copies, waits for them, and re-layouts  1.33 us

profile of v4, /device:TPU:1, one launch (start us, length us, event | category | flops | bytes accessed | tf_op | source)
XLA Modules:
  0.0 56.5 jit_solution(2740464707668489066)
XLA Ops:
  0.0 0.0 copy-start
  0.0 0.0 copy-start.1
  0.0 0.7 %copy-done = f32[8]{0:T(128)S(1)} copy-done((f32[8]{0:T(128)S(1)}, f32[8]{0:T(128)}, u32[]{:S(2)}) %copy-start) | copy-done | bytes 56
  0.7 0.0 copy-done.1
  0.7 55.2 %vcycle.1 = f32[256,128]{1,0:T(8,128)S(1)} custom-call(s32[256,128]{1,0:T(8,128)} %bitcast.4, f32[256,128]{1,0:T(8,128)} %bitcast.5, f32[8]{0:T(128)S(1)} %copy-done, f32[8]{0:T(128)S(1)} %copy-done.1), custom_call_target="tpu_custom_call" | custom-call | tf_op jit(solution)/shard_map/vcycle/pallas_call | solution.py:840
  55.9 0.7 %copy.6 = f32[16,16,128]{2,1,0:T(8,128)} copy(f32[16,16,128]{2,1,0:T(8,128)S(1)} %bitcast.3) | data formatting | bytes 262144
Async XLA Ops:
  0.0 0.7 %copy-start = (f32[8]{0:T(128)S(1)}, f32[8]{0:T(128)}, u32[]{:S(2)}) copy-start(f32[8]{0:T(128)} %refs_2_.1) | copy-start | bytes 100
  0.0 0.7 %copy-start.1 = (f32[8]{0:T(128)S(1)}, f32[8]{0:T(128)}, u32[]{:S(2)}) copy-start(f32[8]{0:T(128)} %refs_3_.1) | copy-start | bytes 100

commit v5 on v4

--- a/solution.py
+++ b/solution.py
@@ -85,10 +85,9 @@
 
 
 def steps_of(count):
-    for s in (8, 4, 2):
-        if count % s == 0:
-            return s
-    return 1
+    if count <= 32:
+        return count
+    return 8 if count % 8 == 0 else 1
 
 
 def prepare(lev):
@@ -753,6 +752,17 @@
     post_copies(lambda c: c.start())
     for z in range(16):
         l0.U[z, 0:16, :] = l0.U[z, 0:16, :] + l0.V[z + 1, 0:16, :]
+    for copy in r1_copies():
+        copy.wait_send()
+    es_lines(lambda c: c.wait_send())
+    for copy in es_planes():
+        copy.wait_send()
+    f1_copies(lambda c: c.wait_send())
+    for copy in f2_copies():
+        copy.wait_send()
+    gather(red, s_red, r_red, lambda c: c.wait_send())
+    spread(es3, s_e3, r_e3, lambda c: c.wait_send())
+    spread(f3, s_f3, r_f3, lambda c: c.wait_send())
     gathered(post_red, s_post, r_post)
     tau = jnp.zeros((16, 128), F32)
     for p in range(ngz - 1):
@@ -771,18 +781,7 @@
             x = own
         out[pl.ds(z, 16, stride=16), :] = l0.U[z, 0:16, :] + OMEGA * x
 
-    for copy in r1_copies():
-        copy.wait_send()
-    es_lines(lambda c: c.wait_send())
-    for copy in es_planes():
-        copy.wait_send()
-    f1_copies(lambda c: c.wait_send())
-    for copy in f2_copies():
-        copy.wait_send()
-    gather(red, s_red, r_red, lambda c: c.wait_send())
     post_copies(lambda c: c.wait_send())
-    spread(es3, s_e3, r_e3, lambda c: c.wait_send())
-    spread(f3, s_f3, r_f3, lambda c: c.wait_send())
 
 
 def solution(mesh):

time: 56.6 us -> 56.1 us (level)
  no operation moved by 1% of the time
where the time goes in v5:
time: 56.1 us; the launch traced here: 56 us
  Pallas kernels  54.7 us (98%)
  local copies, waits for them, and re-layouts  1.33 us (2%)
    pallas_call x1, Pallas kernels, per_device(): pl.pallas_call(lambda *refs: kernel(ngx, ngz, *refs), out_shape=jax.Shape...  54.7 us
    unnamed x5, local copies, waits for them, and re-layouts  1.33 us

profile of v5, /device:TPU:1, one launch (start us, length us, event | category | flops | bytes accessed | tf_op | source)
XLA Modules:
  0.0 56.0 jit_solution(10673508890424531936)
XLA Ops:
  0.0 0.0 copy-start
  0.0 0.0 copy-start.1
  0.0 0.7 %copy-done = f32[8]{0:T(128)S(1)} copy-done((f32[8]{0:T(128)S(1)}, f32[8]{0:T(128)}, u32[]{:S(2)}) %copy-start) | copy-done | bytes 56
  0.7 0.0 copy-done.1
  0.7 54.7 %vcycle.1 = f32[256,128]{1,0:T(8,128)S(1)} custom-call(s32[256,128]{1,0:T(8,128)} %bitcast.4, f32[256,128]{1,0:T(8,128)} %bitcast.5, f32[8]{0:T(128)S(1)} %copy-done, f32[8]{0:T(128)S(1)} %copy-done.1), custom_call_target="tpu_custom_call" | custom-call | tf_op jit(solution)/shard_map/vcycle/pallas_call | solution.py:839
  55.4 0.7 %copy.6 = f32[16,16,128]{2,1,0:T(8,128)} copy(f32[16,16,128]{2,1,0:T(8,128)S(1)} %bitcast.3) | data formatting | bytes 262144
Async XLA Ops:
  0.0 0.7 %copy-start = (f32[8]{0:T(128)S(1)}, f32[8]{0:T(128)}, u32[]{:S(2)}) copy-start(f32[8]{0:T(128)} %refs_2_.1) | copy-start | bytes 100
  0.0 0.7 %copy-start.1 = (f32[8]{0:T(128)S(1)}, f32[8]{0:T(128)}, u32[]{:S(2)}) copy-start(f32[8]{0:T(128)} %refs_3_.1) | copy-start | bytes 100

commit v6 on v5

--- a/solution.py
+++ b/solution.py
@@ -85,7 +85,7 @@
 
 
 def steps_of(count):
-    if count <= 32:
+    if count <= 64:
         return count
     return 8 if count % 8 == 0 else 1
 
@@ -95,7 +95,7 @@
     zero = jnp.zeros((1, X, 128), F32)
     lev.E[0:1] = zero
     lev.E[Z + 1 : Z + 2] = zero
-    (loop if Z // n > 8 else unrolled)(Z // n, lambda i: couplings(lev, i * n, n))
+    unrolled(Z // n, lambda i: couplings(lev, i * n, n))
     lev.WZ[0:1] = zero
     lev.WZ[Z : Z + 1] = zero
     lev.A[Z : Z + 1] = zero

time: 56.1 us -> 55.6 us (level)
  Pallas kernels: 54.7 us -> 54.1 us
where the time goes in v6:
time: 55.6 us; the launch traced here: 55.5 us
  Pallas kernels  54.1 us (97%)
  local copies, waits for them, and re-layouts  1.33 us (2%)
    pallas_call x1, Pallas kernels, per_device(): pl.pallas_call(lambda *refs: kernel(ngx, ngz, *refs), out_shape=jax.Shape...  54.1 us
    unnamed x5, local copies, waits for them, and re-layouts  1.33 us

profile of v6, /device:TPU:1, one launch (start us, length us, event | category | flops | bytes accessed | tf_op | source)
XLA Modules:
  0.0 55.5 jit_solution(5357567783043679260)
XLA Ops:
  0.0 0.0 copy-start
  0.0 0.0 copy-start.1
  0.0 0.7 %copy-done = f32[8]{0:T(128)S(1)} copy-done((f32[8]{0:T(128)S(1)}, f32[8]{0:T(128)}, u32[]{:S(2)}) %copy-start) | copy-done | bytes 56
  0.7 0.0 copy-done.1
  0.7 54.1 %vcycle.1 = f32[256,128]{1,0:T(8,128)S(1)} custom-call(s32[256,128]{1,0:T(8,128)} %bitcast.4, f32[256,128]{1,0:T(8,128)} %bitcast.5, f32[8]{0:T(128)S(1)} %copy-done, f32[8]{0:T(128)S(1)} %copy-done.1), custom_call_target="tpu_custom_call" | custom-call | tf_op jit(solution)/shard_map/vcycle/pallas_call | solution.py:839
  54.8 0.7 %copy.6 = f32[16,16,128]{2,1,0:T(8,128)} copy(f32[16,16,128]{2,1,0:T(8,128)S(1)} %bitcast.3) | data formatting | bytes 262144
Async XLA Ops:
  0.0 0.7 %copy-start = (f32[8]{0:T(128)S(1)}, f32[8]{0:T(128)}, u32[]{:S(2)}) copy-start(f32[8]{0:T(128)} %refs_2_.1) | copy-start | bytes 100
  0.0 0.7 %copy-start.1 = (f32[8]{0:T(128)S(1)}, f32[8]{0:T(128)}, u32[]{:S(2)}) copy-start(f32[8]{0:T(128)} %refs_3_.1) | copy-start | bytes 100

commit v7 on v6

--- a/solution.py
+++ b/solution.py
@@ -343,14 +343,11 @@
             go(1, k, fh.at[0], fr.at[0, gz], gx_at(1))
             go(2, k, fh.at[1], fr.at[1, gz], gx_at(-1))
 
-    def f1_arrive():
-        def get(slot, dst, k):
-            p = gz_at(k)
-            remote(dst, dst, s_f1.at[slot, k], r_f1.at[slot, p], gx, gz_at(1)).wait_recv()
-
-        loop(ngz - 1, lambda k: get(0, f1.at[gz], k + 1))
-        loop(ngz, lambda k: get(1, fr.at[0, gz], k))
-        loop(ngz, lambda k: get(2, fr.at[1, gz], k))
+    def f1_arrive(k):
+        p = gz_at(k)
+        for slot, dst in ((0, f1.at[gz]), (1, fr.at[0, gz]), (2, fr.at[1, gz])):
+            if slot or k:
+                remote(dst, dst, s_f1.at[slot, k], r_f1.at[slot, p], gx, gz_at(1)).wait_recv()
 
     def es_lines(act):
         for k in FAR_FIRST:
@@ -635,15 +632,16 @@
 
     l1.F[:, 8:24, :] = jnp.zeros((l1.Z, 16, 128), F32)
     lane16 = iota((16, 128), 1)
-    f1_arrive()
-    for p in range(ngz):
-        l1.F[p * 8 : p * 8 + 8, 0:8, :] = unpack2(f1[p])
+    for k in FAR_FIRST + (0,):
+        p = gz_at(k)
+        f1_arrive(k)
+        l1.F[pl.ds(p * 8, 8), 0:8, :] = unpack2(f1[p])
         for side, present, row in ((0, has_left, 20), (1, has_right, 8)):
             v = jnp.where(present, fr[side, p], 0.0)
             both = (jnp.where((lane16 & 1) == 0, v, roll(v, 1, 1)), jnp.where((lane16 & 1) == 1, v, roll(v, -1, 1)))
             for zz in range(4):
-                for k in range(2):
-                    l1.F[p * 8 + zz * 2 + k, row : row + 4, :] = both[k][zz * 4 : zz * 4 + 4]
+                for j in range(2):
+                    l1.F[p * 8 + zz * 2 + j, row : row + 4, :] = both[j][zz * 4 : zz * 4 + 4]
     pre(l1)
     coarsen(l1.R, 0, l1, l2, l2.F, 0, True)
     lane8 = iota((8, 8, 128), 2)

time: 55.6 us -> 55.6 us (level)
  no operation moved by 1% of the time
where the time goes in v7:
time: 55.6 us; the launch traced here: 55.5 us
  Pallas kernels  54.2 us (97%)
  local copies, waits for them, and re-layouts  1.33 us (2%)
    pallas_call x1, Pallas kernels, per_device(): pl.pallas_call(lambda *refs: kernel(ngx, ngz, *refs), out_shape=jax.Shape...  54.2 us
    unnamed x5, local copies, waits for them, and re-layouts  1.33 us

profile of v7, /device:TPU:1, one launch (start us, length us, event | category | flops | bytes accessed | tf_op | source)
XLA Modules:
  0.0 55.5 jit_solution(5895988273993906344)
XLA Ops:
  0.0 0.0 copy-start
  0.0 0.0 copy-start.1
  0.0 0.7 %copy-done = f32[8]{0:T(128)S(1)} copy-done((f32[8]{0:T(128)S(1)}, f32[8]{0:T(128)}, u32[]{:S(2)}) %copy-start) | copy-done | bytes 56
  0.7 0.0 copy-done.1
  0.7 54.2 %vcycle.1 = f32[256,128]{1,0:T(8,128)S(1)} custom-call(s32[256,128]{1,0:T(8,128)} %bitcast.4, f32[256,128]{1,0:T(8,128)} %bitcast.5, f32[8]{0:T(128)S(1)} %copy-done, f32[8]{0:T(128)S(1)} %copy-done.1), custom_call_target="tpu_custom_call" | custom-call | tf_op jit(solution)/shard_map/vcycle/pallas_call | solution.py:837
  54.8 0.7 %copy.6 = f32[16,16,128]{2,1,0:T(8,128)} copy(f32[16,16,128]{2,1,0:T(8,128)S(1)} %bitcast.3) | data formatting | bytes 262144
Async XLA Ops:
  0.0 0.7 %copy-start = (f32[8]{0:T(128)S(1)}, f32[8]{0:T(128)}, u32[]{:S(2)}) copy-start(f32[8]{0:T(128)} %refs_2_.1) | copy-start | bytes 100
  0.0 0.7 %copy-start.1 = (f32[8]{0:T(128)S(1)}, f32[8]{0:T(128)}, u32[]{:S(2)}) copy-start(f32[8]{0:T(128)} %refs_3_.1) | copy-start | bytes 100
